TPU v7x, 32 devices: a whole 2x2x4 slice. The times are simulated.
32 devices in a mesh: dp: 8 (over z, core), tensor: 4 (over y, x).
Axes of the slice: x: 2, y: 2, z: 4, core: 2. Of those that a mesh axis runs over, the one named last changes fastest.
Arguments:
- tokens: bfloat16 [8192, 2048], P('dp'), may hold values from -6 to 6
- lengths: int32 [64], P('dp'), may hold values from 1 to 64, 2560 in all
- cotangent: bfloat16 [8192, 2048], P('dp'), may hold values from -6 to 6
- pre_gain: float32 [2048], replicated, may hold values from 0.5 to 1.5
- pre_shift: float32 [2048], replicated, may hold values from -1.5 to 1.5
- qkv_weight: bfloat16 [3, 2048, 2048], P(None, None, 'tensor'), may hold values from -0.125 to 0.125
- qkv_bias: float32 [3, 2048], P(None, 'tensor'), may hold values from -1.5 to 1.5
- mix_gain: float32 [2048], P('tensor'), may hold values from 0.5 to 1.5
- mix_shift: float32 [2048], P('tensor'), may hold values from -1.5 to 1.5
- out_weight: bfloat16 [2048, 2048], P('tensor'), may hold values from -0.125 to 0.125
- out_bias: float32 [2048], replicated, may hold values from -1.5 to 1.5
- ffn_gain: float32 [2048], replicated, may hold values from 0.5 to 1.5
- ffn_shift: float32 [2048], replicated, may hold values from -1.5 to 1.5
- up_weight: bfloat16 [2048, 8192], P(None, 'tensor'), may hold values from -0.125 to 0.125
- up_bias: float32 [8192], P('tensor'), may hold values from -2.5 to 2.5
- hid_gain: float32 [8192], P('tensor'), may hold values from 0.5 to 1.5
- hid_shift: float32 [8192], P('tensor'), may hold values from -1.5 to 1.5
- down_weight: bfloat16 [8192, 2048], P('tensor'), may hold values from -0.0625 to 0.0625
- down_bias: float32 [2048], replicated, may hold values from -1.5 to 1.5
Outputs:
- output: bfloat16 [8192, 2048], P('dp')
- tokens_grad: float32 [8192, 2048], P('dp')
- pre_gain_grad: float32 [2048], replicated
- pre_shift_grad: float32 [2048], replicated
- qkv_weight_grad: float32 [3, 2048, 2048], P(None, 'dp', 'tensor')
- qkv_bias_grad: float32 [3, 2048], P(None, 'tensor')
- mix_gain_grad: float32 [2048], P('tensor')
- mix_shift_grad: float32 [2048], P('tensor')
- out_weight_grad: float32 [2048, 2048], P('tensor', 'dp')
- out_bias_grad: float32 [2048], replicated
- ffn_gain_grad: float32 [2048], replicated
- ffn_shift_grad: float32 [2048], replicated
- up_weight_grad: float32 [2048, 8192], P('dp', 'tensor')
- up_bias_grad: float32 [8192], P('tensor')
- hid_gain_grad: float32 [8192], P('tensor')
- hid_shift_grad: float32 [8192], P('tensor')
- down_weight_grad: float32 [8192, 2048], P('tensor', 'dp')
- down_bias_grad: float32 [2048], replicated
Inputs may be any that keep to these rules, and one draw needn't show every extreme that they name: Caption length of each pair; the lengths sum to 2560 and the longest is 64.
All inputs are finite; a program needn't handle non-finite values. No bound on the sum of `lengths` on one device may be relied on, other than what follows from the above.
Results may differ from a plain program's by a relative error of at most 0.013.
Values sent between devices are 32-bit elements; how exact they have to be, the bound alone decides.
No kernel may reach another device: no remote copies, remote signals or barrier semaphores. Data moves between devices by JAX's collectives and lax.ppermute only.
A program may use at most 256 MiB of HBM per device.

v0:
```python
import math

import jax
import jax.numpy as jnp
from jax import lax
from jax.sharding import PartitionSpec as P

D = 2048
HD = 64
FF = 8192
SLOT = 128
IMG = 64
SCALE_BASE = 512


eps = 1e-05
root_half = 0.7071067811865476
inv_root_two_pi = 0.3989422804014327
masked_score = -1e30


def rounded(value):
    return value.astype(jnp.bfloat16)


def tables():
    place = jnp.arange(SLOT, dtype=jnp.float32)
    index = jnp.arange(HD // 2, dtype=jnp.float32)
    theta = 10000.0 ** (-2.0 * index / HD)
    angle = place[:, None] * theta[None, :]
    zeta = (2.0 * index + 0.4 * HD) / (1.4 * HD)
    growth = zeta[None, :] ** ((place[:, None] - SLOT // 2) / SCALE_BASE)
    return (jnp.cos(angle), jnp.sin(angle), growth)


def rotate(value, cosine, sine, factor):
    shape = value.shape
    pairs = value.reshape(shape[:-1] + (shape[-1] // 2, 2))
    even = pairs[..., 0]
    odd = pairs[..., 1]
    cos_b = cosine[:, None, :]
    sin_b = sine[:, None, :]
    fac_b = factor[:, None, :]
    new_even = (even * cos_b - odd * sin_b) * fac_b
    new_odd = (odd * cos_b + even * sin_b) * fac_b
    return jnp.stack([new_even, new_odd], axis=-1).reshape(shape)


def local_norm(value):
    mean = jnp.mean(value, axis=-1, keepdims=True)
    var = jnp.mean(value * value, axis=-1, keepdims=True) - mean * mean
    inverse = lax.rsqrt(var + eps)
    return ((value - mean) * inverse, inverse)


def local_back(grad, hat, gain, inverse):
    scaled = grad * gain
    return inverse * (
        scaled
        - jnp.mean(scaled, axis=-1, keepdims=True)
        - hat * jnp.mean(scaled * hat, axis=-1, keepdims=True)
    )


def body(
    tokens,
    lengths,
    cotangent,
    pre_gain,
    pre_shift,
    qkv_weight,
    qkv_bias,
    mix_gain,
    mix_shift,
    out_weight,
    out_bias,
    ffn_gain,
    ffn_shift,
    up_weight,
    up_bias,
    hid_gain,
    hid_shift,
    down_weight,
    down_bias,
):
    pairs = lengths.shape[0]
    rows = tokens.shape[0]
    local_width = qkv_weight.shape[2]
    local_heads = local_width // HD
    scale = 1.0 / math.sqrt(HD)
    cosine, sine, growth = tables()
    shrink = 1.0 / growth
    place = jnp.arange(SLOT, dtype=jnp.int32)
    causal = (place[None, :] <= place[:, None])[None, None]
    valid = place[None, None, None, :] < (IMG + lengths)[:, None, None, None]
    allowed = causal & valid
    inputs = tokens.astype(jnp.float32)
    pre_hat, pre_inv = local_norm(inputs)
    first = rounded(pre_hat * pre_gain + pre_shift)
    proj = (
        jnp.einsum("td,cde->cte", first, qkv_weight, preferred_element_type=jnp.float32)
        + qkv_bias[:, None, :]
    )
    shaped = proj.reshape(3, pairs, SLOT, local_heads, HD)
    query = rounded(rotate(shaped[0], cosine, sine, growth))
    key = rounded(rotate(shaped[1], cosine, sine, shrink))
    value = rounded(shaped[2])

    def scores_of():
        raw = jnp.einsum("pqhd,pkhd->phqk", query, key, preferred_element_type=jnp.float32) * scale
        return jnp.where(allowed, raw, masked_score)

    scores = scores_of()
    top = jnp.max(scores, axis=-1, keepdims=True)
    expd = jnp.exp(scores - top)
    total = jnp.sum(expd, axis=-1, keepdims=True)
    probs = expd / total
    log_total = top + jnp.log(total)
    mixed = jnp.einsum(
        "phqk,pkhd->pqhd", rounded(probs), value, preferred_element_type=jnp.float32
    ).reshape(rows, local_width)
    mix_sums = lax.psum((jnp.sum(mixed, 1), jnp.sum(mixed * mixed, 1)), "tensor")
    mix_mean = mix_sums[0] / D
    mix_inv = lax.rsqrt(mix_sums[1] / D - mix_mean * mix_mean + eps)
    mix_hat = (mixed - mix_mean[:, None]) * mix_inv[:, None]
    mix_low = rounded(mix_hat * mix_gain + mix_shift)
    branch = lax.psum(jnp.dot(mix_low, out_weight, preferred_element_type=jnp.float32), "tensor")
    middle = inputs + branch + out_bias
    ffn_hat, ffn_inv = local_norm(middle)
    second = rounded(ffn_hat * ffn_gain + ffn_shift)
    hidden = jnp.dot(second, up_weight, preferred_element_type=jnp.float32) + up_bias
    active = jax.nn.gelu(hidden, approximate=False)
    hid_sums = lax.psum((jnp.sum(active, 1), jnp.sum(active * active, 1)), "tensor")
    hid_mean = hid_sums[0] / FF
    hid_inv = lax.rsqrt(hid_sums[1] / FF - hid_mean * hid_mean + eps)
    hid_hat = (active - hid_mean[:, None]) * hid_inv[:, None]
    hid_low = rounded(hid_hat * hid_gain + hid_shift)
    result = lax.psum(jnp.dot(hid_low, down_weight, preferred_element_type=jnp.float32), "tensor")
    final = middle + result + down_bias
    output = rounded(final)
    upstream = cotangent.astype(jnp.float32)
    down_grad = jnp.einsum("tf,td->fd", hid_low, cotangent, preferred_element_type=jnp.float32)
    down_bias_grad = jnp.sum(upstream, 0)
    hid_back = jnp.einsum("td,fd->tf", cotangent, down_weight, preferred_element_type=jnp.float32)
    hid_gain_grad = jnp.sum(hid_back * hid_hat, 0)
    hid_shift_grad = jnp.sum(hid_back, 0)
    hid_scaled = hid_back * hid_gain
    hid_back_sums = lax.psum((jnp.sum(hid_scaled, 1), jnp.sum(hid_scaled * hid_hat, 1)), "tensor")
    active_grad = hid_inv[:, None] * (
        hid_scaled - hid_back_sums[0][:, None] / FF - hid_hat * hid_back_sums[1][:, None] / FF
    )
    slope = 0.5 * (1.0 + lax.erf(hidden * root_half)) + hidden * inv_root_two_pi * jnp.exp(
        -0.5 * hidden * hidden
    )
    hidden_grad = rounded(active_grad * slope)
    up_grad = jnp.einsum("td,tf->df", second, hidden_grad, preferred_element_type=jnp.float32)
    up_bias_grad = jnp.sum(hidden_grad, 0, dtype=jnp.float32)
    second_grad = lax.psum(
        jnp.einsum("tf,df->td", hidden_grad, up_weight, preferred_element_type=jnp.float32),
        "tensor",
    )
    ffn_gain_grad = jnp.sum(second_grad * ffn_hat, 0)
    ffn_shift_grad = jnp.sum(second_grad, 0)
    middle_grad = upstream + local_back(second_grad, ffn_hat, ffn_gain, ffn_inv)
    branch_low = rounded(middle_grad)
    out_bias_grad = jnp.sum(middle_grad, 0)
    out_grad = jnp.einsum("te,td->ed", mix_low, branch_low, preferred_element_type=jnp.float32)
    mix_back = jnp.einsum("td,ed->te", branch_low, out_weight, preferred_element_type=jnp.float32)
    mix_gain_grad = jnp.sum(mix_back * mix_hat, 0)
    mix_shift_grad = jnp.sum(mix_back, 0)
    mix_scaled = mix_back * mix_gain
    mix_back_sums = lax.psum((jnp.sum(mix_scaled, 1), jnp.sum(mix_scaled * mix_hat, 1)), "tensor")
    mixed_grad = mix_inv[:, None] * (
        mix_scaled - mix_back_sums[0][:, None] / D - mix_hat * mix_back_sums[1][:, None] / D
    )
    mixed_grad = rounded(mixed_grad).reshape(pairs, SLOT, local_heads, HD)
    again = jnp.exp(scores_of() - log_total)
    prob_grad = jnp.einsum("pqhd,pkhd->phqk", mixed_grad, value, preferred_element_type=jnp.float32)
    carried = jnp.sum(again * prob_grad, axis=-1, keepdims=True)
    score_grad = rounded(again * (prob_grad - carried))
    query_grad = (
        jnp.einsum("phqk,pkhd->pqhd", score_grad, key, preferred_element_type=jnp.float32) * scale
    )
    key_grad = (
        jnp.einsum("phqk,pqhd->pkhd", score_grad, query, preferred_element_type=jnp.float32) * scale
    )
    value_grad = jnp.einsum(
        "phqk,pqhd->pkhd", rounded(again), mixed_grad, preferred_element_type=jnp.float32
    )
    query_pre = rotate(query_grad, cosine, -sine, growth)
    key_pre = rotate(key_grad, cosine, -sine, shrink)
    proj_grad = rounded(jnp.stack([query_pre, key_pre, value_grad]).reshape(3, rows, local_width))
    qkv_grad = jnp.einsum("td,cte->cde", first, proj_grad, preferred_element_type=jnp.float32)
    qkv_bias_grad = jnp.sum(proj_grad, 1, dtype=jnp.float32)
    first_grad = lax.psum(
        jnp.einsum("cte,cde->td", proj_grad, qkv_weight, preferred_element_type=jnp.float32),
        "tensor",
    )
    pre_gain_grad = jnp.sum(first_grad * pre_hat, 0)
    pre_shift_grad = jnp.sum(first_grad, 0)
    tokens_grad = middle_grad + local_back(first_grad, pre_hat, pre_gain, pre_inv)
    qkv_part, out_part, up_part, down_part = (
        lax.psum_scatter(qkv_grad, "dp", scatter_dimension=1, tiled=True),
        lax.psum_scatter(out_grad, "dp", scatter_dimension=1, tiled=True),
        lax.psum_scatter(up_grad, "dp", scatter_dimension=0, tiled=True),
        lax.psum_scatter(down_grad, "dp", scatter_dimension=1, tiled=True),
    )
    small = lax.psum(
        (
            pre_gain_grad,
            pre_shift_grad,
            qkv_bias_grad,
            mix_gain_grad,
            mix_shift_grad,
            out_bias_grad,
            ffn_gain_grad,
            ffn_shift_grad,
            up_bias_grad,
            hid_gain_grad,
            hid_shift_grad,
            down_bias_grad,
        ),
        "dp",
    )
    return (
        output,
        tokens_grad,
        small[0],
        small[1],
        qkv_part,
        small[2],
        small[3],
        small[4],
        out_part,
        small[5],
        small[6],
        small[7],
        up_part,
        small[8],
        small[9],
        small[10],
        down_part,
        small[11],
    )


def solution(mesh):
    in_specs = (
        P("dp", None),
        P("dp"),
        P("dp", None),
        P(),
        P(),
        P(None, None, "tensor"),
        P(None, "tensor"),
        P("tensor"),
        P("tensor"),
        P("tensor", None),
        P(),
        P(),
        P(),
        P(None, "tensor"),
        P("tensor"),
        P("tensor"),
        P("tensor"),
        P("tensor", None),
        P(),
    )
    out_specs = (
        P("dp", None),
        P("dp", None),
        P(),
        P(),
        P(None, "dp", "tensor"),
        P(None, "tensor"),
        P("tensor"),
        P("tensor"),
        P("tensor", "dp"),
        P(),
        P(),
        P(),
        P("dp", "tensor"),
        P("tensor"),
        P("tensor"),
        P("tensor"),
        P("tensor", "dp"),
        P(),
    )
    return jax.shard_map(body, mesh=mesh, in_specs=in_specs, out_specs=out_specs, check_vma=False)
```

profile of v0, /device:TPU:0, one launch (start us, length us, event | category | flops | bytes accessed | tf_op | source)
XLA Modules:
  0.0 1522.1 jit_solution(11128239787350795962)
XLA Ops:
  10.9 11.5 add_bitcast_fusion
  65.7 11.5 all-reduce.4
  84.9 171.4 %all-reduce.11.cloned.1.call-done = f32[1024,2048]{1,0:T(8,128)} async-done(((f32[1024,2048]{1,0:T(8,128)}), f32[1024,2048]{1,0:T(8,128)}) %all-reduce.11.cloned.1.call-update) | async-done | bytes 8388624 | tf_op jit(solution)/shard_map/psum | solution.py:127
  262.0 36.0 %fusion.57 = (f32[1024]{0:T(1024)S(1)}, f32[1024]{0:T(1024)S(1)}, f32[1024,2048]{1,0:T(8,128)}, f32[1024,2048]{1,0:T(8,128)}) fusion(f32[2048]{0:T(1024)S(1)} %copy-done.37, bf16[2048,2048]{1,0:T(8,128)(2,1)} %param.32, f32[1024,2048]{1,0:T(8,128)S(1)} %get-tuple-element.105, f32[2048]{0:T(1024)S(1)} %copy-done.44, f32[2048]{0:T(1024)S(1)} %copy-done.30, ...), kind=kOutput, calls=%fused_computation.139 | convolution fusion | flops 8743024640 | bytes 33595392 | tf_op jit(solution)/shard_map/dot_general | solution.py:131
  298.0 9.8 all-reduce.3
  307.8 17.3 %multiply_reduce_fusion = (f32[2048]{0:T(1024)}, f32[1024]{0:T(1024)S(1)}, f32[1024]{0:T(1024)S(1)}, f32[2048]{0:T(1024)}, f32[1024,2048]{1,0:T(8,128)}) fusion(f32[1024,2048]{1,0:T(8,128)} %get-tuple-element.104, f32[1024]{0:T(1024)S(1)} %get-tuple-element.126, f32[1024]{0:T(1024)S(1)} %get-tuple-element.125, f32[2048]{0:T(1024)S(1)} %copy-done.38, ...), kind=kOutput, calls=%fused_computation.29 | convolution fusion | flops 8608802816 | bytes 29401088 | tf_op jit(solution)/shard_map/td,fd->tf/dot_general | solution.py:144
  333.2 12.3 convert_reduce_fusion.2
  347.5 13.2 fusion.68
  361.4 15.9 %fusion.56 = f32[1024,2048]{1,0:T(8,128)} fusion(bf16[2048,2048]{1,0:T(8,128)(2,1)} %param.36, f32[1024,2048]{1,0:T(8,128)} %get-tuple-element.104, f32[2048]{0:T(1024)S(1)} %copy-done.43, f32[2048]{0:T(1024)S(1)} %copy-done.38, f32[1024]{0:T(1024)S(1)} %get-tuple-element.126, f32[1024]{0:T(1024)S(1)} %get-tuple-element.125), kind=kOutput, calls=%fused_computation.138 | convolution fusion | flops 8600420352 | bytes 25190400 | tf_op jit(solution)/shard_map/dot_general | solution.py:138
  377.4 155.8 %all-reduce.13.cloned.1.call-done = f32[1024,2048]{1,0:T(8,128)} async-done(((f32[1024,2048]{1,0:T(8,128)}), f32[1024,2048]{1,0:T(8,128)}) %all-reduce.13.cloned.1.call-update) | async-done | bytes 8388624 | tf_op jit(solution)/shard_map/psum | solution.py:158
  533.1 8.3 multiply_reduce_fusion.1
  554.8 9.8 all-reduce.1
  597.8 11.4 convolution_bitcast_fusion.1
  610.7 12.5 convolution_bitcast_fusion
  635.9 280.1 %all-reduce.17.cloned.1.call-done = (f32[1024,2048]{1,0:T(8,128)}, f32[1024,2048]{1,0:T(8,128)}) async-done(((f32[1024,2048]{1,0:T(8,128)}, f32[1024,2048]{1,0:T(8,128)}), (f32[1024,2048]{1,0:T(8,128)}, f32[1024,2048]{1,0:T(8,128)})) %all-reduce.17.cloned.1.call-update) | async-done | bytes 16777232 | tf_op jit(solution)/shard_map/psum | solution.py:138
  923.2 17.5 %fusion.55 = f32[2048,2048]{1,0:T(8,128)} fusion(bf16[1024,2048]{1,0:T(8,128)(2,1)} %param.21, f32[1024,2048]{1,0:T(8,128)} %get-tuple-element.104, f32[2048]{0:T(1024)S(1)} %copy-done.43, f32[2048]{0:T(1024)S(1)} %copy-done.38, f32[1024]{0:T(1024)S(1)} %get-tuple-element.126, f32[1024]{0:T(1024)S(1)} %get-tuple-element.125), kind=kOutput, calls=%fused_computation.137 | convolution fusion | flops 8600420352 | bytes 29384704 | tf_op jit(solution)/shard_map/tf,td->fd/dot_general | solution.py:142
  941.5 16.4 %fusion.53 = f32[2048,2048]{1,0:T(8,128)} fusion(bf16[1024,2048]{1,0:T(8,128)(2,1)} %copy-done.14, f32[1024,2048]{1,0:T(8,128)} %copy-done.2, f32[2048]{0:T(1024)S(1)} %copy-done.45, f32[2048]{0:T(1024)S(1)} %copy-done.30, f32[1024]{0:T(1024)S(1)} %get-tuple-element.128, f32[1024]{0:T(1024)S(1)} %get-tuple-element.127), kind=kOutput, calls=%fused_computation.135 | convolution fusion | flops 8600420352 | bytes 29384704 | tf_op jit(solution)/shard_map/td,tf->df/dot_general | solution.py:156
  958.6 10.4 add_convert_fusion
  969.0 9.7 fusion.17
  978.7 69.7 %reduce-scatter.5.cloned.1.call-done = f32[3,256,512]{1,2,0:T(8,128)} async-done(((f32[3,2048,512]{1,2,0:T(8,128)}), f32[3,256,512]{1,2,0:T(8,128)}) %reduce-scatter.5.cloned.1.call-update) | async-done | bytes 1572880 | tf_op jit(solution)/shard_map/reduce_scatter | solution.py:203
  1051.4 48.1 %reduce-scatter.7.cloned.1.call-done = f32[512,256]{1,0:T(8,128)} async-done(((f32[512,2048]{1,0:T(8,128)}), f32[512,256]{1,0:T(8,128)}) %reduce-scatter.7.cloned.1.call-update) | async-done | bytes 524304 | tf_op jit(solution)/shard_map/reduce_scatter | solution.py:204
  1099.5 56.9 %all-reduce.15.cloned.1.call-done = (f32[2048]{0:T(1024)}, f32[2048]{0:T(1024)}, f32[3,512]{1,0:T(4,128)}, f32[512]{0:T(512)}, f32[512]{0:T(512)}, /*index=5*/f3...) async-done(((f32[2048]{0:T(1024)}, f32[2048]{0:T(1024)}, f32[3,512]{1,0:T(4,128)}, ...) | async-done | bytes 83984 | tf_op jit(solution)/shard_map/psum | solution.py:208
  1156.4 173.4 %reduce-scatter.11.cloned.1.call-done = f32[2048,256]{1,0:T(8,128)} async-done(((f32[2048,2048]{1,0:T(8,128)}), f32[2048,256]{1,0:T(8,128)}) %reduce-scatter.11.cloned.1.call-update) | async-done | bytes 2097168 | tf_op jit(solution)/shard_map/reduce_scatter | solution.py:206
  1329.8 169.6 %reduce-scatter.9.cloned.1.call-done = f32[256,2048]{1,0:T(8,128)} async-done(((f32[2048,2048]{1,0:T(8,128)}), f32[256,2048]{1,0:T(8,128)}) %reduce-scatter.9.cloned.1.call-update) | async-done | bytes 2097168 | tf_op jit(solution)/shard_map/reduce_scatter | solution.py:205
  (193 shorter events, 158.2 us)
Async XLA Ops:
  7.2 70.1 %copy-start = (bf16[512,2048]{1,0:T(8,128)(2,1)S(1)}, bf16[512,2048]{1,0:T(8,128)(2,1)}, u32[]{:S(2)}) copy-start(bf16[512,2048]{1,0:T(8,128)(2,1)} %param.28) | copy-start | bytes 6291460
  7.2 249.1 %all-reduce.11.cloned.1.call-start = ((), (), s32[]{:S(2)}) async-start(), calls=%async_computation.4 | async-start | bytes 16777216 | tf_op jit(solution)/shard_map/psum | solution.py:127
  10.9 11.6 copy-start.26
  10.9 11.6 copy-start.28
  41.7 12.0 copy-start.8
  57.1 20.2 %copy-start.40 = (f32[512]{0:T(512)S(1)}, f32[512]{0:T(512)}, u32[]{:S(2)}) copy-start(f32[512]{0:T(512)} %param.26) | copy-start | bytes 6148
  57.1 20.2 %copy-start.46 = (f32[512]{0:T(512)S(1)}, f32[512]{0:T(512)}, u32[]{:S(2)}) copy-start(f32[512]{0:T(512)} %param.27) | copy-start | bytes 6148
  77.3 179.0 %copy-start.36 = (f32[2048]{0:T(1024)S(1)}, f32[2048]{0:T(1024)}, u32[]{:S(2)}) copy-start(f32[2048]{0:T(1024)} %param.29) | copy-start | bytes 24580
  84.8 177.2 %copy-start.30 = (f32[2048]{0:T(1024)S(1)}, f32[2048]{0:T(1024)}, u32[]{:S(2)}) copy-start(f32[2048]{0:T(1024)} %param.30) | copy-start | bytes 24580
  84.8 177.2 %copy-start.37 = (f32[2048]{0:T(1024)S(1)}, f32[2048]{0:T(1024)}, u32[]{:S(2)}) copy-start(f32[2048]{0:T(1024)} %param.33) | copy-start | bytes 24580
  84.8 177.2 %copy-start.44 = (f32[2048]{0:T(1024)S(1)}, f32[2048]{0:T(1024)}, u32[]{:S(2)}) copy-start(f32[2048]{0:T(1024)} %param.31) | copy-start | bytes 24580
  84.8 448.3 %all-reduce.13.cloned.1.call-start = ((), (), s32[]{:S(2)}) async-start(), calls=%async_computation.5 | async-start | bytes 16777216 | tf_op jit(solution)/shard_map/psum | solution.py:158
  261.9 36.0 %copy-start.2 = (f32[1024,2048]{1,0:T(8,128)}, f32[1024,2048]{1,0:T(8,128)S(1)}, u32[]{:S(2)}) copy-start(f32[1024,2048]{1,0:T(8,128)S(1)} %get-tuple-element.105) | copy-start | bytes 25165828
  262.0 45.8 %copy-start.38 = (f32[2048]{0:T(1024)S(1)}, f32[2048]{0:T(1024)}, u32[]{:S(2)}) copy-start(f32[2048]{0:T(1024)} %param.34) | copy-start | bytes 24580
  360.8 555.3 %all-reduce.17.cloned.1.call-start = ((), (), s32[]{:S(2)}) async-start(), calls=%async_computation.11 | async-start | bytes 33554432 | tf_op jit(solution)/shard_map/psum | solution.py:138
  533.1 9.4 copy-start.13
  584.8 10.5 copy-start.18
  609.2 439.2 %reduce-scatter.5.cloned.1.call-start = ((), (), s32[]{:S(2)}) async-start(), calls=%async_computation.6 | async-start | bytes 14155776 | tf_op jit(solution)/shard_map/reduce_scatter | solution.py:203
  623.2 476.3 %reduce-scatter.7.cloned.1.call-start = ((), (), s32[]{:S(2)}) async-start(), calls=%async_computation.7 | async-start | bytes 4718592 | tf_op jit(solution)/shard_map/reduce_scatter | solution.py:204
  633.1 523.3 %all-reduce.15.cloned.1.call-start = ((), (), s32[]{:S(2)}) async-start(), calls=%async_computation.10 | async-start | bytes 172032 | tf_op jit(solution)/shard_map/psum | solution.py:208
  923.2 406.6 %reduce-scatter.11.cloned.1.call-start = ((), (), s32[]{:S(2)}) async-start(), calls=%async_computation.9 | async-start | bytes 18874368 | tf_op jit(solution)/shard_map/reduce_scatter | solution.py:206
  940.8 558.6 %reduce-scatter.9.cloned.1.call-start = ((), (), s32[]{:S(2)}) async-start(), calls=%async_computation.8 | async-start | bytes 18874368 | tf_op jit(solution)/shard_map/reduce_scatter | solution.py:205
  958.6 10.4 copy-start.5
  969.0 545.8 %copy-start.1 = (bf16[512,2048]{1,0:T(8,128)(2,1)S(1)}, bf16[512,2048]{1,0:T(8,128)(2,1)}, u32[]{:S(2)}) copy-start(bf16[512,2048]{1,0:T(8,128)(2,1)} %param.28) | copy-start | bytes 6291460
  (33 other events, 147.8 us)
Sparse Core Ops, SparseCore 0:
  84.9 171.3 all-reduce.10
  360.9 172.1 all-reduce.12
  609.4 306.6 all-reduce.16
  918.2 130.1 reduce-scatter.4
  1051.1 48.3 reduce-scatter.6
  1104.5 51.8 all-reduce.14
  1159.3 170.4 reduce-scatter.10
  1332.8 166.6 reduce-scatter.8
where the time goes:
time: 1530 us; the launch traced here: 1520 us
  waiting for transfers between devices  1130 us (74%)
  matrix products  185 us (12%)
  other arithmetic  82.8 us (5%)
  local copies, waits for them, and re-layouts  73.6 us (5%)
  blocking collectives  39.2 us (3%)
  between operations  15.4 us (1%)
    psum x1, waiting for transfers between devices, body(): lax.psum(jnp.dot(hid_low, down_weight, preferred_element_type=jnp.float32...  280 us
    reduce_scatter x1, waiting for transfers between devices, body(): lax.psum_scatter(down_grad, 'dp', scatter_dimension=1, tiled=True)  173 us
    psum x1, waiting for transfers between devices, body(): lax.psum(jnp.dot(mix_low, out_weight, preferred_element_type=jnp.float32)...  171 us
    reduce_scatter x1, waiting for transfers between devices, body(): lax.psum_scatter(up_grad, 'dp', scatter_dimension=0, tiled=True)  170 us
    psum x1, waiting for transfers between devices, body(): lax.psum(jnp.einsum('tf,df->td', hidden_grad, up_weight, preferred_elemen...  156 us
    reduce_scatter x1, waiting for transfers between devices, body(): lax.psum_scatter(qkv_grad, 'dp', scatter_dimension=1, tiled=True)  69.7 us
    psum x1, waiting for transfers between devices, body(): lax.psum((pre_gain_grad, pre_shift_grad, qkv_bias_grad, mix_gain_grad, mi...  56.9 us
    reduce_scatter x1, waiting for transfers between devices, body(): lax.psum_scatter(out_grad, 'dp', scatter_dimension=1, tiled=True)  48.1 us
  transfers between devices with their start and end apart: 8, of which 8 were waited for; matrix products, arithmetic and copies ran while one was open for 7% of the time, Pallas kernels for 0%

commit v1 on v0

v1 whole, which is shorter than its diff:
```python
import functools
import math

import jax
import jax.numpy as jnp
import numpy as np
from jax import lax
from jax.experimental import pallas as pl
from jax.experimental.pallas import tpu as pltpu
from jax.sharding import PartitionSpec as P

D = 2048
HD = 64
FF = 8192
SLOT = 128
IMG = 64
SCALE_BASE = 512
LANES = 128

eps = 1e-05
root_half = 0.7071067811865476
inv_root_two_pi = 0.3989422804014327
masked_score = -1e30
scale = 1.0 / math.sqrt(HD)
bf16 = jnp.bfloat16
f32 = jnp.float32


def rounded(value):
    return value.astype(bf16)


def tables():
    place = np.arange(SLOT, dtype=np.float64)[:, None]
    index = (np.arange(LANES) % HD) // 2
    theta = 10000.0 ** (-2.0 * index / HD)
    angle = place * theta[None, :]
    zeta = (2.0 * index + 0.4 * HD) / (1.4 * HD)
    growth = zeta[None, :] ** ((place - SLOT // 2) / SCALE_BASE)
    sign = np.where(np.arange(LANES) % 2 == 0, -1.0, 1.0)[None, :]
    cosine, sine = np.cos(angle), np.sin(angle) * sign
    return np.stack(
        [cosine * growth, sine * growth, cosine / growth, sine / growth]
    ).astype(np.float32)


def norm_kernel(t_ref, x_ref, gain_ref, shift_ref, o_ref):
    value = x_ref[...].astype(f32)
    mean = jnp.mean(value, axis=-1, keepdims=True)
    var = jnp.mean(value * value, axis=-1, keepdims=True) - mean * mean
    hat = (value - mean) * lax.rsqrt(var + eps)
    o_ref[...] = rounded(hat * gain_ref[...] + shift_ref[...])


def pre_norm(tensor_at, tokens, gain, shift, n, chunk):
    rows = n * SLOT
    return pl.pallas_call(
        norm_kernel,
        out_shape=jax.ShapeDtypeStruct((rows, D), bf16),
        grid_spec=pltpu.PrefetchScalarGridSpec(
            num_scalar_prefetch=1,
            grid=(n,),
            in_specs=[
                pl.BlockSpec((SLOT, D), lambda p, t: (chunk * n + lax.bitwise_xor(p, t[0]), 0)),
                pl.BlockSpec((1, D), lambda p, t: (0, 0)),
                pl.BlockSpec((1, D), lambda p, t: (0, 0)),
            ],
            out_specs=pl.BlockSpec((SLOT, D), lambda p, t: (p, 0)),
        ),
        cost_estimate=pl.CostEstimate(
            flops=8 * rows * D, bytes_accessed=4 * rows * D, transcendentals=0
        ),
        name="pre_norm",
    )(tensor_at, tokens, gain.reshape(1, D), shift.reshape(1, D))


def copy_kernel(t_ref, x_ref, o_ref):
    o_ref[...] = x_ref[...]


def permuted(tensor_at, value, n):
    rows = value.shape[0]
    return pl.pallas_call(
        copy_kernel,
        out_shape=jax.ShapeDtypeStruct(value.shape, value.dtype),
        grid_spec=pltpu.PrefetchScalarGridSpec(
            num_scalar_prefetch=1,
            grid=(rows // SLOT,),
            in_specs=[
                pl.BlockSpec((SLOT, D), lambda i, t: (lax.bitwise_xor(i, t[0]), 0)),
            ],
            out_specs=pl.BlockSpec((SLOT, D), lambda i, t: (i, 0)),
        ),
        cost_estimate=pl.CostEstimate(flops=0, bytes_accessed=4 * rows * D, transcendentals=0),
        name="reorder",
    )(tensor_at, value)


def partner(value, even):
    return jnp.where(
        even, pltpu.roll(value, LANES - 1, axis=1), pltpu.roll(value, 1, axis=1)
    )


def two_heads(value, low_half):
    zero = jnp.zeros_like(value)
    return jnp.concatenate([jnp.where(low_half, value, zero), jnp.where(low_half, zero, value)], 0)


def contract(left, right, dims):
    return lax.dot_general(left, right, (dims, ((), ())), preferred_element_type=f32)


def softmax_two(query, keys, allowed):
    scores = contract(query, keys, ((1,), (1,)))
    halves = []
    for head in range(2):
        part = jnp.where(allowed, scores[:, head * SLOT : (head + 1) * SLOT], masked_score)
        top = jnp.max(part, axis=-1, keepdims=True)
        expd = jnp.exp(part - top)
        halves.append(expd * (1.0 / jnp.sum(expd, axis=-1, keepdims=True)))
    return halves


def masks(length):
    lane = lax.broadcasted_iota(jnp.int32, (SLOT, LANES), 1)
    row = lax.broadcasted_iota(jnp.int32, (SLOT, LANES), 0)
    allowed = (lane <= row) & (lane < IMG + length)
    return lane % 2 == 0, lane < HD, allowed


def attend_kernel(n, chunk, t_ref, len_ref, proj_ref, tab_ref, qkv_ref, mixed_ref, stat_ref):
    p = pl.program_id(0)
    length = len_ref[chunk * n + lax.bitwise_xor(p, t_ref[0])]
    even, low_half, allowed = masks(length)
    width = proj_ref.shape[2]
    total = jnp.zeros((SLOT, 1), f32)
    squares = jnp.zeros((SLOT, 1), f32)
    for at in range(0, width, LANES):
        cols = slice(at, at + LANES)
        q_raw = proj_ref[0, :, cols]
        k_raw = proj_ref[1, :, cols]
        query = rounded(q_raw * tab_ref[0] + partner(q_raw, even) * tab_ref[1]) * bf16(scale)
        key = rounded(k_raw * tab_ref[2] + partner(k_raw, even) * tab_ref[3])
        value = rounded(proj_ref[2, :, cols])
        qkv_ref[0, :, cols] = query
        qkv_ref[1, :, cols] = key
        qkv_ref[2, :, cols] = value
        probs = jnp.concatenate(
            [rounded(v) for v in softmax_two(query, two_heads(key, low_half), allowed)], 1
        )
        mixed = contract(probs, two_heads(value, low_half), ((1,), (0,)))
        mixed_ref[:, cols] = mixed
        total = total + jnp.sum(mixed, axis=-1, keepdims=True)
        squares = squares + jnp.sum(mixed * mixed, axis=-1, keepdims=True)
    lane = lax.broadcasted_iota(jnp.int32, (SLOT, LANES), 1)
    both = jnp.where(lane == 0, total, jnp.where(lane == 1, squares, 0.0))
    stat_ref[...] = both.T[:8]


def attend(tensor_at, lengths, proj, tabs, n, chunk):
    rows, width = proj.shape[1:]
    heads = width // HD
    return pl.pallas_call(
        functools.partial(attend_kernel, n, chunk),
        out_shape=(
            jax.ShapeDtypeStruct((3, rows, width), bf16),
            jax.ShapeDtypeStruct((rows, width), f32),
            jax.ShapeDtypeStruct((8, rows), f32),
        ),
        grid_spec=pltpu.PrefetchScalarGridSpec(
            num_scalar_prefetch=2,
            grid=(n,),
            in_specs=[
                pl.BlockSpec((3, SLOT, width), lambda p, t, l: (0, p, 0)),
                pl.BlockSpec((4, SLOT, LANES), lambda p, t, l: (0, 0, 0)),
            ],
            out_specs=[
                pl.BlockSpec((3, SLOT, width), lambda p, t, l: (0, p, 0)),
                pl.BlockSpec((SLOT, width), lambda p, t, l: (p, 0)),
                pl.BlockSpec((8, SLOT), lambda p, t, l: (0, p)),
            ],
        ),
        cost_estimate=pl.CostEstimate(
            flops=8 * rows * SLOT * width,
            bytes_accessed=22 * rows * width,
            transcendentals=rows * SLOT * heads,
        ),
        name="attend",
    )(tensor_at, lengths, proj, tabs)


def attend_back_kernel(n, chunk, t_ref, len_ref, qkv_ref, grad_ref, tab_ref, out_ref):
    p = pl.program_id(0)
    length = len_ref[chunk * n + lax.bitwise_xor(p, t_ref[0])]
    even, low_half, allowed = masks(length)
    width = grad_ref.shape[1]
    for at in range(0, width, LANES):
        cols = slice(at, at + LANES)
        query = qkv_ref[0, :, cols]
        key = qkv_ref[1, :, cols]
        value = qkv_ref[2, :, cols]
        grad = grad_ref[:, cols]
        keys = two_heads(key, low_half)
        probs = softmax_two(query, keys, allowed)
        prob_grads = contract(grad, two_heads(value, low_half), ((1,), (1,)))
        score_grads = []
        for head in range(2):
            own = prob_grads[:, head * SLOT : (head + 1) * SLOT]
            carried = jnp.sum(probs[head] * own, axis=-1, keepdims=True)
            score_grads.append(rounded(probs[head] * (own - carried)))
        score_grad = jnp.concatenate(score_grads, 1)
        prob_low = jnp.concatenate([rounded(v) for v in probs], 1)
        query_grad = contract(score_grad, keys, ((1,), (0,))) * scale
        key_both = contract(score_grad, query, ((0,), (0,)))
        key_grad = jnp.where(low_half, key_both[:SLOT], key_both[SLOT:])
        value_both = contract(prob_low, grad, ((0,), (0,)))
        value_grad = jnp.where(low_half, value_both[:SLOT], value_both[SLOT:])
        out_ref[0, :, cols] = rounded(
            query_grad * tab_ref[0] - partner(query_grad, even) * tab_ref[1]
        )
        out_ref[1, :, cols] = rounded(
            key_grad * tab_ref[2] - partner(key_grad, even) * tab_ref[3]
        )
        out_ref[2, :, cols] = rounded(value_grad)


def attend_back(tensor_at, lengths, qkv, grad, tabs, n, chunk):
    rows, width = grad.shape
    heads = width // HD
    return pl.pallas_call(
        functools.partial(attend_back_kernel, n, chunk),
        out_shape=jax.ShapeDtypeStruct((3, rows, width), bf16),
        grid_spec=pltpu.PrefetchScalarGridSpec(
            num_scalar_prefetch=2,
            grid=(n,),
            in_specs=[
                pl.BlockSpec((3, SLOT, width), lambda p, t, l: (0, p, 0)),
                pl.BlockSpec((SLOT, width), lambda p, t, l: (p, 0)),
                pl.BlockSpec((4, SLOT, LANES), lambda p, t, l: (0, 0, 0)),
            ],
            out_specs=pl.BlockSpec((3, SLOT, width), lambda p, t, l: (0, p, 0)),
        ),
        cost_estimate=pl.CostEstimate(
            flops=20 * rows * SLOT * width,
            bytes_accessed=14 * rows * width,
            transcendentals=rows * SLOT * heads,
        ),
        name="attend_back",
    )(tensor_at, lengths, qkv, grad, tabs)


def gather_kernel(layout, t_ref, *refs):
    out_ref = refs[-1]
    at = 0
    for place, parts in enumerate(layout):
        where = place if t_ref is None else lax.bitwise_xor(place, t_ref[0])
        left = 0
        for _ in range(parts):
            part = refs[at][...]
            out_ref[where, :, left : left + part.shape[1]] = part.astype(out_ref.dtype)
            left += part.shape[1]
            at += 1


def assembled(blocks):
    n = len(blocks)
    flat = [part for parts in blocks for part in parts]
    tile = 32
    out = pl.pallas_call(
        functools.partial(gather_kernel, [len(parts) for parts in blocks], None),
        out_shape=jax.ShapeDtypeStruct((n, SLOT, D), bf16),
        grid=(SLOT // tile,),
        in_specs=[pl.BlockSpec((tile, part.shape[1]), lambda i: (i, 0)) for part in flat],
        out_specs=pl.BlockSpec((n, tile, D), lambda i: (0, i, 0)),
        cost_estimate=pl.CostEstimate(
            flops=n * SLOT * D, bytes_accessed=6 * n * SLOT * D, transcendentals=0
        ),
        name="assemble",
    )(*flat)
    return out.reshape(n * SLOT, D)


def placed(tensor_at, blocks, chunk, chunks, dtype, before):
    n = len(blocks)
    flat = [part for parts in blocks for part in parts]
    tile = 32
    layout = [len(parts) for parts in blocks]
    extra = [] if before is None else [before]

    def kernel(t_ref, *refs):
        gather_kernel(layout, t_ref, *refs[: len(flat)], refs[-1])

    return pl.pallas_call(
        kernel,
        out_shape=jax.ShapeDtypeStruct((chunks * n, SLOT, D), dtype),
        grid_spec=pltpu.PrefetchScalarGridSpec(
            num_scalar_prefetch=1,
            grid=(SLOT // tile,),
            in_specs=[pl.BlockSpec((tile, part.shape[1]), lambda i, t: (i, 0)) for part in flat]
            + [pl.BlockSpec(memory_space=pl.ANY)] * len(extra),
            out_specs=pl.BlockSpec((n, tile, D), lambda i, t: (chunk, i, 0)),
        ),
        input_output_aliases={1 + len(flat): 0} if extra else {},
        cost_estimate=pl.CostEstimate(
            flops=n * SLOT * D, bytes_accessed=8 * n * SLOT * D, transcendentals=0
        ),
        name="place",
    )(tensor_at, *flat, *extra)


class Links:
    def __init__(self, n, dp):
        self.n, self.dp = n, dp
        self.last = ()

    def swap(self, value, mask, axis="tensor"):
        size = self.n if axis == "tensor" else self.dp
        return lax.ppermute(value, axis, [(i, i ^ mask) for i in range(size)])

    def bits(self, size):
        return [1 << b for b in range(size.bit_length() - 1)]

    def then(self, *values):
        flat, tree = jax.tree.flatten(values)
        flat = lax.optimization_barrier(tuple(flat) + self.last)[: len(flat)]
        values = jax.tree.unflatten(tree, flat)
        return values[0] if len(values) == 1 else values

    def mark(self, *values):
        self.last = tuple(jax.tree.leaves(values))

    def exchange(self, value):
        return [value] + [self.swap(value, mask) for mask in range(1, self.n)]

    def summed(self, held):
        ordered = []
        for mask, value in enumerate(held):
            blocks = [value[:, (p ^ mask) * SLOT : ((p ^ mask) + 1) * SLOT] for p in range(self.n)]
            ordered.append(jnp.concatenate(blocks, 1) if mask else value)
        while len(ordered) > 1:
            ordered = [ordered[i] + ordered[i + 1] for i in range(0, len(ordered), 2)]
        return ordered[0]

    def spread(self, value, axis):
        for mask in self.bits(self.n if axis == "tensor" else self.dp):
            value = value + self.swap(value, mask, axis)
        return value

    def halves(self):
        order = self.bits(self.n)
        if self.n == 4:
            return [(0, D // 2, order), (D // 2, D, order[::-1])]
        return [(0, D, order)]


class Scatter:
    def __init__(self, links, parts):
        self.links, self.at = links, 0
        self.held = [
            {p: [full[p * SLOT : (p + 1) * SLOT]] for p in range(links.n)} for full in parts
        ]
        self.send()

    def send(self):
        self.came, sents = [], []
        for held, (_, _, order) in zip(self.held, self.links.halves()):
            mask = order[self.at]
            away = [p for p in sorted(held) if p & mask]
            sent = [functools.reduce(jnp.add, held.pop(p)) for p in away]
            sent = sent[0] if len(sent) == 1 else jnp.concatenate(sent, 0)
            sents.append(sent)
            self.came.append((away, mask, self.links.swap(sent, mask)))
        self.links.mark(sents)

    def take(self):
        values = self.links.then([came for _, _, came in self.came])
        for held, (away, mask, _), came in zip(self.held, self.came, values):
            for i, p in enumerate(away):
                held[p ^ mask].append(came[i * SLOT : (i + 1) * SLOT])
        self.at += 1

    def step(self):
        while self.at + 1 < len(self.links.halves()[0][2]):
            self.take()
            self.send()

    def finish(self):
        self.take()
        result = [functools.reduce(jnp.add, held[0]) for held in self.held]
        return result[0] if len(result) == 1 else jnp.concatenate(result, 1)


class Gather:
    def __init__(self, links, own):
        self.links, self.own = links, own
        links.mark(own)
        if links.n == 4:
            self.one, self.two = links.swap(own, 1), links.swap(own, 2)

    def step(self):
        if self.links.n == 4:
            one, two = self.links.then(self.one, self.two)
            left, right = two[:, : D // 2], one[:, D // 2 :]
            self.links.mark(left, right)
            self.three = [self.links.swap(left, 1), self.links.swap(right, 2)]

    def result(self):
        if self.links.n == 4:
            three = self.links.then(self.three)
            return [[self.own], [self.one], [self.two], three]
        held = {0: self.own}
        for mask in self.links.bits(self.links.n):
            held.update({p | mask: self.links.swap(v, mask) for p, v in held.items()})
        return [[held[p]] for p in range(self.links.n)]


def local_norm(value):
    mean = jnp.mean(value, axis=-1, keepdims=True)
    var = jnp.mean(value * value, axis=-1, keepdims=True) - mean * mean
    inverse = lax.rsqrt(var + eps)
    return ((value - mean) * inverse, inverse)


def local_back(grad, hat, gain, inverse):
    scaled = grad * gain
    return inverse * (
        scaled
        - jnp.mean(scaled, axis=-1, keepdims=True)
        - hat * jnp.mean(scaled * hat, axis=-1, keepdims=True)
    )


def matmul(left, right):
    return jnp.dot(left, right, preferred_element_type=f32)


def joined(pieces):
    if len(pieces) == 1:
        return pieces[0]
    return jnp.concatenate(lax.optimization_barrier(tuple(pieces)), -2)


def make_body(n, dp):
    links = Links(n, dp)

    def body(
        tokens,
        lengths,
        cotangent,
        pre_gain,
        pre_shift,
        qkv_weight,
        qkv_bias,
        mix_gain,
        mix_shift,
        out_weight,
        out_bias,
        ffn_gain,
        ffn_shift,
        up_weight,
        up_bias,
        hid_gain,
        hid_shift,
        down_weight,
        down_bias,
    ):
        at = lax.axis_index("tensor").astype(jnp.int32)
        tensor_at = at.reshape(1)
        tabs = jnp.asarray(tables())
        rows = n * SLOT
        chunks = tokens.shape[0] // rows
        each = range(chunks)

        def own_rows(value, c):
            return lax.dynamic_slice_in_dim(value, (c * n + at) * SLOT, SLOT, 0).astype(f32)

        def columns(weight):
            return [weight[:, a:b] for a, b, _ in links.halves()]

        first, qkv, mixed, stats = [], [], [], []
        for c in each:
            first.append(pre_norm(tensor_at, tokens, pre_gain, pre_shift, n, c))
            proj = (
                jnp.einsum("td,cde->cte", first[c], qkv_weight, preferred_element_type=f32)
                + qkv_bias[:, None, :]
            )
            held, mix, stat = attend(tensor_at, lengths, proj, tabs, n, c)
            qkv.append(held)
            mixed.append(mix)
            stats.append(links.exchange(stat))
        links.mark(mixed[-1])
        mix_low, mix_hat, mix_inv, branch = [], [], [], []
        for c in each:
            stat = links.summed(links.then(stats[c]))
            mean = stat[0] / D
            inverse = lax.rsqrt(stat[1] / D - mean * mean + eps)
            hat = (mixed[c] - mean[:, None]) * inverse[:, None]
            low = rounded(hat * mix_gain + mix_shift)
            mix_hat.append(hat)
            mix_inv.append(inverse)
            mix_low.append(low)
            branch.append(Scatter(links, [matmul(low, w) for w in columns(out_weight)]))
        cot = permuted(tensor_at, links.then(cotangent), n)
        hid_back = []
        for c in each:
            back = jnp.einsum(
                "td,fd->tf", cot[c * rows : (c + 1) * rows], down_weight, preferred_element_type=f32
            )
            links.mark(back)
            hid_back.append(back)
            branch[c].step()

        middle, ffn_hat, ffn_inv, second = [], [], [], []
        for c in each:
            own = own_rows(tokens, c) + branch[c].finish() + out_bias
            hat, inverse = local_norm(own)
            middle.append(own)
            ffn_hat.append(hat)
            ffn_inv.append(inverse)
            second.append(Gather(links, hat * ffn_gain + ffn_shift))
        for c in each:
            second[c].step()
        hidden, active, scaled, erf, sums = [], [], [], [], []
        for c in each:
            second[c] = assembled(second[c].result())
            hidden.append(matmul(second[c], up_weight) + up_bias)
            erf.append(lax.erf(hidden[c] * root_half))
            active.append(hidden[c] * (0.5 * (1.0 + erf[c])))
            scaled.append(hid_back[c] * hid_gain)
            own = jnp.stack(
                [
                    jnp.sum(active[c], 1),
                    jnp.sum(active[c] * active[c], 1),
                    jnp.sum(scaled[c], 1),
                    jnp.sum(scaled[c] * active[c], 1),
                ]
            )
            links.mark(own)
            sums.append(links.exchange(own))
        hid_low, hidden_grad, second_grad = [], [], []
        hid_gain_grad, hid_shift_grad, up_bias_grad = 0.0, 0.0, 0.0
        for c in each:
            own = links.summed(links.then(sums[c]))
            mean = own[0] / FF
            inverse = lax.rsqrt(own[1] / FF - mean * mean + eps)
            plain = own[2] / FF
            against = inverse * (own[3] / FF - mean * plain)
            hat = (active[c] - mean[:, None]) * inverse[:, None]
            low = rounded(hat * hid_gain + hid_shift)
            slope = 0.5 * (1.0 + erf[c]) + hidden[c] * inv_root_two_pi * jnp.exp(
                -0.5 * hidden[c] * hidden[c]
            )
            grad = inverse[:, None] * (scaled[c] - plain[:, None] - hat * against[:, None])
            grad = rounded(grad * slope)
            hid_gain_grad = hid_gain_grad + jnp.sum(hid_back[c] * hat, 0)
            hid_shift_grad = hid_shift_grad + jnp.sum(hid_back[c], 0)
            up_bias_grad = up_bias_grad + jnp.sum(grad, 0, dtype=f32)
            links.mark(low, grad)
            hid_low.append(low)
            hidden_grad.append(grad)
            if c == chunks - 1:
                down_grad = jnp.einsum(
                    "tf,td->fd", links.then(joined(hid_low)), cot, preferred_element_type=f32
                )
                links.mark(down_grad)
                down_part = lax.psum_scatter(down_grad, "dp", scatter_dimension=1, tiled=True)
            grad = links.then(grad)
            second_grad.append(
                Scatter(
                    links,
                    [
                        jnp.einsum("tf,df->td", grad, up_weight[a:b], preferred_element_type=f32)
                        for a, b, _ in links.halves()
                    ],
                )
            )
        second_grad[0].step()
        up_grad = jnp.einsum(
            "td,tf->df",
            links.then(joined(second)),
            joined(hidden_grad),
            preferred_element_type=f32,
        )
        links.mark(up_grad)
        up_part = lax.psum_scatter(up_grad, "dp", scatter_dimension=0, tiled=True)
        for grad in second_grad[1:]:
            grad.step()

        middle_grad, branch_low, result = [], [], []
        ffn_gain_grad, ffn_shift_grad, out_bias_grad, down_bias_grad = 0.0, 0.0, 0.0, 0.0
        for c in each:
            upstream = own_rows(cotangent, c)
            own = second_grad[c].finish()
            ffn_gain_grad = ffn_gain_grad + jnp.sum(own * ffn_hat[c], 0)
            ffn_shift_grad = ffn_shift_grad + jnp.sum(own, 0)
            grad = upstream + local_back(own, ffn_hat[c], ffn_gain, ffn_inv[c])
            out_bias_grad = out_bias_grad + jnp.sum(grad, 0)
            down_bias_grad = down_bias_grad + jnp.sum(upstream, 0)
            middle_grad.append(grad)
            branch_low.append(Gather(links, grad))
            low = links.then(hid_low[c])
            parts = [matmul(low, w) for w in columns(down_weight)]
            links.mark(parts)
            result.append(parts)
            branch_low[c].step()
        mix_gain_grad, mix_shift_grad, qkv_bias_grad = 0.0, 0.0, 0.0
        proj_grad, first_grad, sums, mix_scaled = [], [], [], []
        for c in each:
            branch_low[c] = assembled(branch_low[c].result())
            result[c] = Scatter(links, result[c])
            back = jnp.einsum("td,ed->te", branch_low[c], out_weight, preferred_element_type=f32)
            mix_gain_grad = mix_gain_grad + jnp.sum(back * mix_hat[c], 0)
            mix_shift_grad = mix_shift_grad + jnp.sum(back, 0)
            mix_scaled.append(back * mix_gain)
            own = jnp.stack([jnp.sum(mix_scaled[c], 1), jnp.sum(mix_scaled[c] * mix_hat[c], 1)])
            links.mark(own)
            sums.append(links.exchange(own))
        out_grad = jnp.einsum(
            "te,td->ed",
            joined(mix_low),
            links.then(joined(branch_low)),
            preferred_element_type=f32,
        )
        links.mark(out_grad)
        out_part = lax.psum_scatter(out_grad, "dp", scatter_dimension=1, tiled=True)
        for c in each:
            own = links.summed(links.then(sums[c]))
            grad = mix_inv[c][:, None] * (
                mix_scaled[c] - own[0][:, None] / D - mix_hat[c] * own[1][:, None] / D
            )
            grads = attend_back(tensor_at, lengths, qkv[c], rounded(grad), tabs, n, c)
            proj_grad.append(grads)
            qkv_bias_grad = qkv_bias_grad + jnp.sum(grads, 1, dtype=f32)
            first_grad.append(
                Scatter(
                    links,
                    [
                        jnp.einsum(
                            "cte,cde->td", grads, qkv_weight[:, a:b], preferred_element_type=f32
                        )
                        for a, b, _ in links.halves()
                    ],
                )
            )
        qkv_grad = jnp.einsum(
            "td,cte->cde",
            joined(first),
            links.then(joined(proj_grad)),
            preferred_element_type=f32,
        )
        links.mark(qkv_grad)
        qkv_part = lax.psum_scatter(qkv_grad, "dp", scatter_dimension=1, tiled=True)

        for c in each:
            result[c].step()
        for c in each:
            first_grad[c].step()
        outputs, grads = [], []
        pre_gain_grad, pre_shift_grad = 0.0, 0.0
        for c in each:
            outputs.append(Gather(links, middle[c] + result[c].finish() + down_bias))
        for c in each:
            hat, inverse = local_norm(own_rows(tokens, c))
            own = first_grad[c].finish()
            pre_gain_grad = pre_gain_grad + jnp.sum(own * hat, 0)
            pre_shift_grad = pre_shift_grad + jnp.sum(own, 0)
            grads.append(Gather(links, middle_grad[c] + local_back(own, hat, pre_gain, inverse)))
        for c in each:
            outputs[c].step()
        for c in each:
            grads[c].step()
        output, tokens_grad = None, None
        for c in each:
            output = placed(tensor_at, outputs[c].result(), c, chunks, bf16, output)
        for c in each:
            tokens_grad = placed(tensor_at, grads[c].result(), c, chunks, f32, tokens_grad)

        whole = links.spread(
            jnp.concatenate([ffn_gain_grad, ffn_shift_grad, out_bias_grad, down_bias_grad]),
            "tensor",
        )
        parts = [
            whole,
            up_bias_grad,
            hid_gain_grad,
            hid_shift_grad,
            mix_gain_grad,
            mix_shift_grad,
        ]
        early = links.spread(jnp.concatenate(parts), "dp")
        early = jnp.split(early, np.cumsum([D, D, D] + [p.shape[0] for p in [whole[:D]] + parts[1:-1]]))
        whole = links.spread(jnp.concatenate([pre_gain_grad, pre_shift_grad]), "tensor")
        late = links.spread(jnp.concatenate([whole, qkv_bias_grad.reshape(-1)]), "dp")
        return (
            output.reshape(tokens.shape),
            tokens_grad.reshape(tokens.shape),
            late[:D],
            late[D : 2 * D],
            qkv_part,
            late[2 * D :].reshape(qkv_bias.shape),
            early[7],
            early[8],
            out_part,
            early[2],
            early[0],
            early[1],
            up_part,
            early[4],
            early[5],
            early[6],
            down_part,
            early[3],
        )

    return body


def solution(mesh):
    in_specs = (
        P("dp", None),
        P("dp"),
        P("dp", None),
        P(),
        P(),
        P(None, None, "tensor"),
        P(None, "tensor"),
        P("tensor"),
        P("tensor"),
        P("tensor", None),
        P(),
        P(),
        P(),
        P(None, "tensor"),
        P("tensor"),
        P("tensor"),
        P("tensor"),
        P("tensor", None),
        P(),
    )
    out_specs = (
        P("dp", None),
        P("dp", None),
        P(),
        P(),
        P(None, "dp", "tensor"),
        P(None, "tensor"),
        P("tensor"),
        P("tensor"),
        P("tensor", "dp"),
        P(),
        P(),
        P(),
        P("dp", "tensor"),
        P("tensor"),
        P("tensor"),
        P("tensor"),
        P("tensor", "dp"),
        P(),
    )
    body = make_body(mesh.shape["tensor"], mesh.shape["dp"])
    return jax.shard_map(body, mesh=mesh, in_specs=in_specs, out_specs=out_specs, check_vma=False)
```

time: 1530 us -> 1020 us (0.67)
  waiting for transfers between devices: 1130 us -> 542 us
  starting transfers between devices: 0.8 us -> 108 us
  Pallas kernels: 0 us -> 88.9 us
  local copies, waits for them, and re-layouts: 73.6 us -> 33.8 us
  blocking collectives: 39.2 us -> 0 us
  other arithmetic: 82.8 us -> 59.7 us
  matrix products: 185 us -> 164 us
    psum x4 -> x0, waiting for transfers between devices: 664 us -> none  [the longest x1 280 us: body(): lax.psum(jnp.dot(hid_low, down_weight, preferred_element_type=jnp.float32...]
    ppermute x0 -> x92, waiting for transfers between devices: none -> 306 us  [swap(): return lax.ppermute(value, axis, [(i, i ^ mask) for i in range(size)])]
    reduce_scatter x3, waiting for transfers between devices: 287 us -> 169 us  [the longest x1 169 us: body(): up_part = lax.psum_scatter(up_grad, 'dp', scatter_dimension=0, tiled=True)]
    reduce_scatter x1, waiting for transfers between devices: 173 us -> 64.7 us  [body(): lax.psum_scatter(down_grad, 'dp', scatter_dimension=1, tiled=True)]
    ppermute x0 -> x92, starting transfers between devices: none -> 107 us  [swap(): return lax.ppermute(value, axis, [(i, i ^ mask) for i in range(size)])]
    pallas_call x0 -> x15, Pallas kernels: none -> 88.9 us  [the longest x2 23.1 us: attend_back(): pl.pallas_call(functools.partial(attend_back_kernel, n, chunk), out_shape...]
    psum x4 -> x0, blocking collectives: 39.2 us -> none  [the longest x1 11.5 us: body(): lax.psum((jnp.sum(mixed, 1), jnp.sum(mixed * mixed, 1)), 'tensor')]
    reduce_sum x6 -> x11, other arithmetic: 39.1 us -> 17.9 us  [the longest x2 9.47 us: body(): hid_shift_grad = hid_shift_grad + jnp.sum(hid_back[c], 0)]
  transfers between devices with their start and end apart: 8 -> 96, of which waited for: 8 -> 36; matrix products, arithmetic and copies ran while one was open for 7% -> 22% of each run, Pallas kernels for 0% -> 6%
where the time goes in v1:
time: 1020 us; the launch traced here: 1010 us
  waiting for transfers between devices  542 us (53%)
  matrix products  164 us (16%)
  starting transfers between devices  108 us (11%)
  Pallas kernels  88.9 us (9%)
  other arithmetic  59.7 us (6%)
  local copies, waits for them, and re-layouts  33.8 us (3%)
  between operations  16.4 us (2%)
    ppermute x92, waiting for transfers between devices, swap(): return lax.ppermute(value, axis, [(i, i ^ mask) for i in range(size)])  306 us
    reduce_scatter x1, waiting for transfers between devices, body(): up_part = lax.psum_scatter(up_grad, 'dp', scatter_dimension=0, tiled=True)  169 us
    ppermute x92, starting transfers between devices, swap(): return lax.ppermute(value, axis, [(i, i ^ mask) for i in range(size)])  107 us
    reduce_scatter x1, waiting for transfers between devices, body(): lax.psum_scatter(down_grad, 'dp', scatter_dimension=1, tiled=True)  64.7 us
    dot_general x10, matrix products, matmul(): return jnp.dot(left, right, preferred_element_type=f32)  41 us
    pallas_call x2, Pallas kernels, attend_back(): pl.pallas_call(functools.partial(attend_back_kernel, n, chunk), out_shape...  23.1 us
    dot_general x4, matrix products, body(): jnp.einsum('tf,df->td', grad, up_weight[a:b], preferred_element_type=f32)  21.2 us
  transfers between devices with their start and end apart: 96, of which 36 were waited for; matrix products, arithmetic and copies ran while one was open for 22% of the time, Pallas kernels for 6%

profile of v1, /device:TPU:0, one launch (start us, length us, event | category | flops | bytes accessed | tf_op | source)
XLA Modules:
  0.0 1012.2 jit_solution(8414355364544392216)
XLA Ops:
  77.0 10.7 %fusion.40 = f32[512,2048]{1,0:T(8,128)} fusion(bf16[2048,2048]{1,0:T(8,128)(2,1)} %param.37, bf16[1024,2048]{1,0:T(8,128)(2,1)} %reorder.1), kind=kOutput, calls=%fused_computation.70 | convolution fusion | flops 4294967296 | bytes 14680064 | tf_op jit(solution)/shard_map/td,fd->tf/dot_general | solution.py:507
  87.7 9.6 fusion.42
  140.7 12.5 %collective-permute-done.17.refs_2_ = f32[128,2048]{1,0:T(8,128)S(1)} collective-permute-done((f32[128,2048]{1,0:T(8,128)S(1)}, f32[128,2048]{1,0:T(8,128)S(1)}, u32[]{:S(2)}, u32[]{:S(2)}) %collective-permute-start.17) | collective-permute-done | bytes 1048608 | tf_op jit(solution)/shard_map/ppermute | solution.py:319
  158.5 17.2 %collective-permute-done.15.refs_2_ = f32[128,2048]{1,0:T(8,128)S(1)} collective-permute-done((f32[128,2048]{1,0:T(8,128)S(1)}, f32[128,2048]{1,0:T(8,128)S(1)}, u32[]{:S(2)}, u32[]{:S(2)}) %collective-permute-start.15) | collective-permute-done | bytes 1048608 | tf_op jit(solution)/shard_map/ppermute | solution.py:319
  194.3 11.2 %multiply_reduce_fusion.7 = (f32[512]{0:T(512)S(1)}, f32[512]{0:T(512)S(1)}, f32[512]{0:T(512)S(1)}, f32[512]{0:T(512)S(1)}, f32[512,2048]{1,0:T(8,128)}, /*index=5*/f32[512,2048]{1,0:T(8,128)}) fusion(f32[512,2048]{1,0:T(8,128)} %fusion.40, f32[2048]{0:T(1024)S(1)} %copy-done.94, f32[2048]{0:T(1024)S(1)} %copy-done.95, bf16[512,2048]{1,0:T(8,128)(2,1)} %bitcast.99, ...), kind=kOutput, calls=%fused_computation.55 | convolution fusion | flops 4307548160 | bytes 23093248 | tf_op jit(solution)/shard_map/dot_general | solution.py:435
  214.8 9.8 multiply_reduce_fusion.6
  259.3 11.8 %fusion.171 = f32[2048,2048]{1,0:T(8,128)} fusion(bf16[1024,2048]{1,0:T(8,128)(2,1)S(1)} %pad_maximum_fusion, bf16[1024,2048]{1,0:T(8,128)(2,1)S(1)} %copy-done.38), kind=kOutput, calls=%fused_computation.330 | convolution fusion | flops 8589934592 | bytes 25165824 | tf_op jit(solution)/shard_map/tf,td->fd/dot_general | solution.py:563
  292.6 11.9 %fusion.10 = f32[2048,2048]{1,0:T(8,128)} fusion(bf16[1024,2048]{1,0:T(8,128)(2,1)S(1)} %copy-done.39, bf16[512,2048]{1,0:T(8,128)(2,1)S(1)} %copy-done.65, bf16[512,2048]{1,0:T(8,128)(2,1)S(1)} %copy-done.64), kind=kOutput, calls=%fused_computation.15 | convolution fusion | flops 8598323200 | bytes 25165824 | tf_op jit(solution)/shard_map/td,tf->df/dot_general | solution.py:579
  423.0 11.5 %attend_back.2 = bf16[3,512,512]{2,1,0:T(8,128)(2,1)} custom-call(s32[1]{0:T(128)} %bitcast.t_ref, s32[8]{0:T(128)} %len_ref.7, bf16[3,512,512]{2,1,0:T(8,128)(2,1)} %get-tuple-element.194.qkv_ref, bf16[512,512]{1,0:T(8,128)(2,1)} %multiply_convert_fusion.1.grad_ref, f32[4,128,128]{2,1,0:T(8,128)} %constant.68.clone.tab_ref), custom_call_target="tpu_custom_call" | custom-call | flops 671088640 | bytes 3670016 | tf_op jit(solution)/shard_map/attend_back/pallas_call | solution.py:231
  446.7 11.7 %attend_back.3 = bf16[3,512,512]{2,1,0:T(8,128)(2,1)} custom-call(s32[1]{0:T(128)} %bitcast.t_ref, s32[8]{0:T(128)} %len_ref.7, bf16[3,512,512]{2,1,0:T(8,128)(2,1)} %get-tuple-element.210.qkv_ref, bf16[512,512]{1,0:T(8,128)(2,1)} %multiply_convert_fusion.grad_ref, f32[4,128,128]{2,1,0:T(8,128)} %constant.68.clone.tab_ref), custom_call_target="tpu_custom_call" | custom-call | flops 671088640 | bytes 3670016 | tf_op jit(solution)/shard_map/attend_back/pallas_call | solution.py:231
  472.0 9.4 convolution_bitcast_fusion
  489.5 24.0 %collective-permute-done.87 = f32[8192]{0:T(1024)S(1)} collective-permute-done((f32[8192]{0:T(1024)S(1)}, f32[8192]{0:T(1024)S(1)}, u32[]{:S(2)}, u32[]{:S(2)}) %collective-permute-start.87) | collective-permute-done | bytes 32800 | tf_op jit(solution)/shard_map/ppermute | solution.py:319
  520.9 19.4 %collective-permute-done.38 = f32[256,1024]{1,0:T(8,128)S(1)} collective-permute-done((f32[256,1024]{1,0:T(8,128)S(1)}, f32[256,1024]{1,0:T(8,128)S(1)}, u32[]{:S(2)}, u32[]{:S(2)}) %collective-permute-start.38) | collective-permute-done | bytes 1048608 | tf_op jit(solution)/shard_map/ppermute | solution.py:319
  544.0 20.7 %collective-permute-done.61 = f32[256,1024]{1,0:T(8,128)S(1)} collective-permute-done((f32[256,1024]{1,0:T(8,128)S(1)}, f32[256,1024]{1,0:T(8,128)S(1)}, u32[]{:S(2)}, u32[]{:S(2)}) %collective-permute-start.61) | collective-permute-done | bytes 1048608 | tf_op jit(solution)/shard_map/ppermute | solution.py:319
  566.4 18.8 %collective-permute-done.58 = f32[256,1024]{1,0:T(8,128)S(1)} collective-permute-done((f32[256,1024]{1,0:T(8,128)S(1)}, f32[256,1024]{1,0:T(8,128)S(1)}, u32[]{:S(2)}, u32[]{:S(2)}) %collective-permute-start.58) | collective-permute-done | bytes 1048608 | tf_op jit(solution)/shard_map/ppermute | solution.py:319
  595.5 11.4 %collective-permute-done.56 = f32[128,1024]{1,0:T(8,128)S(1)} collective-permute-done((f32[128,1024]{1,0:T(8,128)S(1)}, f32[128,1024]{1,0:T(8,128)S(1)}, u32[]{:S(2)}, u32[]{:S(2)}) %collective-permute-start.56) | collective-permute-done | bytes 524320 | tf_op jit(solution)/shard_map/ppermute | solution.py:319
  612.3 9.4 collective-permute-done.68
  624.1 8.8 collective-permute-done.66
  640.7 16.7 %collective-permute-done.83 = f32[4096]{0:T(1024)S(1)} collective-permute-done((f32[4096]{0:T(1024)S(1)}, f32[4096]{0:T(1024)S(1)}, u32[]{:S(2)}, u32[]{:S(2)}) %collective-permute-start.83) | collective-permute-done | bytes 16416 | tf_op jit(solution)/shard_map/ppermute | solution.py:319
  665.1 17.4 %collective-permute-done.64.refs_1_ = f32[128,2048]{1,0:T(8,128)S(1)} collective-permute-done((f32[128,2048]{1,0:T(8,128)S(1)}, f32[128,2048]{1,0:T(8,128)S(1)}, u32[]{:S(2)}, u32[]{:S(2)}) %collective-permute-start.64) | collective-permute-done | bytes 1048608 | tf_op jit(solution)/shard_map/ppermute | solution.py:319
  691.5 13.5 %collective-permute-done.74.refs_1_ = f32[128,2048]{1,0:T(8,128)S(1)} collective-permute-done((f32[128,2048]{1,0:T(8,128)}, f32[128,2048]{1,0:T(8,128)S(1)}, u32[]{:S(2)}, u32[]{:S(2)}) %collective-permute-start.74) | collective-permute-done | bytes 1048608 | tf_op jit(solution)/shard_map/ppermute | solution.py:319
  712.4 15.0 %collective-permute-done.72.refs_1_ = f32[128,2048]{1,0:T(8,128)S(1)} collective-permute-done((f32[128,2048]{1,0:T(8,128)S(1)}, f32[128,2048]{1,0:T(8,128)S(1)}, u32[]{:S(2)}, u32[]{:S(2)}) %collective-permute-start.72) | collective-permute-done | bytes 1048608 | tf_op jit(solution)/shard_map/ppermute | solution.py:319
  771.1 64.7 %reduce-scatter.11.cloned.1.call-done = f32[2048,256]{1,0:T(8,128)} async-done(((f32[2048,2048]{1,0:T(8,128)}), f32[2048,256]{1,0:T(8,128)}) %reduce-scatter.11.cloned.1.call-update) | async-done | bytes 2097168 | tf_op jit(solution)/shard_map/reduce_scatter | solution.py:567
  835.8 169.4 %reduce-scatter.9.cloned.1.call-done = f32[256,2048]{1,0:T(8,128)} async-done(((f32[2048,2048]{1,0:T(8,128)}), f32[256,2048]{1,0:T(8,128)}) %reduce-scatter.9.cloned.1.call-update) | async-done | bytes 2097168 | tf_op jit(solution)/shard_map/reduce_scatter | solution.py:586
  (637 shorter events, 459.3 us)
Async XLA Ops:
  7.2 760.8 %reduce-scatter.5.cloned.1.call-start = ((), (), s32[]{:S(2)}) async-start(), calls=%async_computation.4 | async-start | bytes 14155776 | tf_op jit(solution)/shard_map/reduce_scatter | solution.py:653
  67.7 40.7 %collective-permute-start.7 = (f32[256,1024]{1,0:T(8,128)}, f32[256,1024]{1,0:T(8,128)}, u32[]{:S(2)}, u32[]{:S(2)}) collective-permute-start(f32[256,1024]{1,0:T(8,128)} %concatenate.219), channel_id=1, source_target_pairs={{0,2},{1,3},{2,0},{3,1},{4,6},{5,7},{6,4},{7,5},{8,10},{9,11},{10,... | collective-permute-start | bytes 3145736 | tf_op jit(solution)/shard_map/ppermute | solution.py:319
  69.4 42.0 %collective-permute-start.6 = (f32[256,1024]{1,0:T(8,128)}, f32[256,1024]{1,0:T(8,128)}, u32[]{:S(2)}, u32[]{:S(2)}) collective-permute-start(f32[256,1024]{1,0:T(8,128)} %pad_maximum_fusion.5), channel_id=1, source_target_pairs={{0,1},{1,0},{2,3},{3,2},{4,5},{5,4},{6,7},{7,6},{8,9},{9,8},{10,11... | collective-permute-start | bytes 3145736 | tf_op jit(solution)/shard_map/ppermute | solution.py:319
  138.7 40.1 %collective-permute-start.14 = (f32[128,2048]{1,0:T(8,128)S(1)}, f32[128,2048]{1,0:T(8,128)S(1)}, u32[]{:S(2)}, u32[]{:S(2)}) collective-permute-start(f32[128,2048]{1,0:T(8,128)S(1)} %multiply_add_fusion.refs_0_), channel_id=1, source_target_pairs={{0,1},{1,0},{2,3},{3,2},{4,5},{5,4},{6,7},{7,6},{8,9},{9,8},{10,11... | collective-permute-start | bytes 3145736 | tf_op jit(solution)/shard_map/ppermute | solution.py:319
  248.0 38.6 %collective-permute-start.31 = (f32[256,1024]{1,0:T(8,128)}, f32[256,1024]{1,0:T(8,128)S(1)}, u32[]{:S(2)}, u32[]{:S(2)}) collective-permute-start(f32[256,1024]{1,0:T(8,128)} %concatenate.220), channel_id=1, source_target_pairs={{0,2},{1,3},{2,0},{3,1},{4,6},{5,7},{6,4},{7,5},{8,10},{9,11},{10,... | collective-permute-start | bytes 3145736 | tf_op jit(solution)/shard_map/ppermute | solution.py:319
  313.7 42.0 %collective-permute-start.33 = (f32[128,1024]{1,0:T(8,128)S(1)}, f32[128,1024]{1,0:T(8,128)S(1)}, u32[]{:S(2)}, u32[]{:S(2)}) collective-permute-start(f32[128,1024]{1,0:T(8,128)S(1)} %slice_add_fusion.19), channel_id=1, source_target_pairs={{0,1},{1,0},{2,3},{3,2},{4,5},{5,4},{6,7},{7,6},{8,9},{9,8},{10,11... | collective-permute-start | bytes 1572872 | tf_op jit(solution)/shard_map/ppermute | solution.py:319
  315.5 40.2 %collective-permute-start.32 = (f32[128,1024]{1,0:T(8,128)S(1)}, f32[128,1024]{1,0:T(8,128)S(1)}, u32[]{:S(2)}, u32[]{:S(2)}) collective-permute-start(f32[128,1024]{1,0:T(8,128)S(1)} %slice_add_fusion.20), channel_id=1, source_target_pairs={{0,2},{1,3},{2,0},{3,1},{4,6},{5,7},{6,4},{7,5},{8,10},{9,11},{10,... | collective-permute-start | bytes 1572872 | tf_op jit(solution)/shard_map/ppermute | solution.py:319
  481.4 289.7 %reduce-scatter.7.cloned.1.call-start = ((), (), s32[]{:S(2)}) async-start(), calls=%async_computation.5 | async-start | bytes 4718592 | tf_op jit(solution)/shard_map/reduce_scatter | solution.py:626
  482.2 353.6 %reduce-scatter.11.cloned.1.call-start = ((), (), s32[]{:S(2)}) async-start(), calls=%async_computation.7 | async-start | bytes 18874368 | tf_op jit(solution)/shard_map/reduce_scatter | solution.py:567
  483.0 522.3 %reduce-scatter.9.cloned.1.call-start = ((), (), s32[]{:S(2)}) async-start(), calls=%async_computation.6 | async-start | bytes 18874368 | tf_op jit(solution)/shard_map/reduce_scatter | solution.py:586
  518.0 46.7 %collective-permute-start.61 = (f32[256,1024]{1,0:T(8,128)S(1)}, f32[256,1024]{1,0:T(8,128)S(1)}, u32[]{:S(2)}, u32[]{:S(2)}) collective-permute-start(f32[256,1024]{1,0:T(8,128)S(1)} %copy-done.83), channel_id=1, source_target_pairs={{0,2},{1,3},{2,0},{3,1},{4,6},{5,7},{6,4},{7,5},{8,10},{9,11},{10,... | collective-permute-start | bytes 3145736 | tf_op jit(solution)/shard_map/ppermute | solution.py:319
  518.7 46.1 %collective-permute-start.60 = (f32[256,1024]{1,0:T(8,128)S(1)}, f32[256,1024]{1,0:T(8,128)S(1)}, u32[]{:S(2)}, u32[]{:S(2)}) collective-permute-start(f32[256,1024]{1,0:T(8,128)S(1)} %copy-done.82), channel_id=1, source_target_pairs={{0,1},{1,0},{2,3},{3,2},{4,5},{5,4},{6,7},{7,6},{8,9},{9,8},{10,11... | collective-permute-start | bytes 3145736 | tf_op jit(solution)/shard_map/ppermute | solution.py:319
  540.2 44.9 %collective-permute-start.58 = (f32[256,1024]{1,0:T(8,128)S(1)}, f32[256,1024]{1,0:T(8,128)S(1)}, u32[]{:S(2)}, u32[]{:S(2)}) collective-permute-start(f32[256,1024]{1,0:T(8,128)S(1)} %copy-done.84), channel_id=1, source_target_pairs={{0,1},{1,0},{2,3},{3,2},{4,5},{5,4},{6,7},{7,6},{8,9},{9,8},{10,11... | collective-permute-start | bytes 3145736 | tf_op jit(solution)/shard_map/ppermute | solution.py:319
  542.3 44.4 %collective-permute-start.59 = (f32[256,1024]{1,0:T(8,128)S(1)}, f32[256,1024]{1,0:T(8,128)S(1)}, u32[]{:S(2)}, u32[]{:S(2)}) collective-permute-start(f32[256,1024]{1,0:T(8,128)S(1)} %concatenate.225), channel_id=1, source_target_pairs={{0,2},{1,3},{2,0},{3,1},{4,6},{5,7},{6,4},{7,5},{8,10},{9,11},{10,... | collective-permute-start | bytes 3145736 | tf_op jit(solution)/shard_map/ppermute | solution.py:319
  542.4 51.8 %collective-permute-start.57 = (f32[128,1024]{1,0:T(8,128)S(1)}, f32[128,1024]{1,0:T(8,128)S(1)}, u32[]{:S(2)}, u32[]{:S(2)}) collective-permute-start(f32[128,1024]{1,0:T(8,128)S(1)} %slice_add_fusion.13), channel_id=1, source_target_pairs={{0,1},{1,0},{2,3},{3,2},{4,5},{5,4},{6,7},{7,6},{8,9},{9,8},{10,11... | collective-permute-start | bytes 1572872 | tf_op jit(solution)/shard_map/ppermute | solution.py:319
  564.7 42.5 %collective-permute-start.55 = (f32[128,1024]{1,0:T(8,128)S(1)}, f32[128,1024]{1,0:T(8,128)S(1)}, u32[]{:S(2)}, u32[]{:S(2)}) collective-permute-start(f32[128,1024]{1,0:T(8,128)S(1)} %slice_add_fusion.11), channel_id=1, source_target_pairs={{0,1},{1,0},{2,3},{3,2},{4,5},{5,4},{6,7},{7,6},{8,9},{9,8},{10,11... | collective-permute-start | bytes 1572872 | tf_op jit(solution)/shard_map/ppermute | solution.py:319
  564.8 44.1 %collective-permute-start.54 = (f32[128,1024]{1,0:T(8,128)S(1)}, f32[128,1024]{1,0:T(8,128)S(1)}, u32[]{:S(2)}, u32[]{:S(2)}) collective-permute-start(f32[128,1024]{1,0:T(8,128)S(1)} %slice_add_fusion.12), channel_id=1, source_target_pairs={{0,2},{1,3},{2,0},{3,1},{4,6},{5,7},{6,4},{7,5},{8,10},{9,11},{10,... | collective-permute-start | bytes 1572872 | tf_op jit(solution)/shard_map/ppermute | solution.py:319
  586.7 47.3 %collective-permute-start.90 = (f32[15360]{0:T(1024)S(1)}, f32[15360]{0:T(1024)S(1)}, u32[]{:S(2)}, u32[]{:S(2)}) collective-permute-start(f32[15360]{0:T(1024)S(1)} %add.629), channel_id=1, source_target_pairs={{0,8},{4,12},{8,0},{12,4},{16,24},{20,28},{24,16},{28,20},{1,9},{5... | collective-permute-start | bytes 184328 | tf_op jit(solution)/shard_map/ppermute | solution.py:319
  610.8 50.1 %collective-permute-start.63 = (f32[128,2048]{1,0:T(8,128)}, f32[128,2048]{1,0:T(8,128)}, u32[]{:S(2)}, u32[]{:S(2)}) collective-permute-start(f32[128,2048]{1,0:T(8,128)} %fusion.91.refs_0_), channel_id=1, source_target_pairs={{0,2},{1,3},{2,0},{3,1},{4,6},{5,7},{6,4},{7,5},{8,10},{9,11},{10,... | collective-permute-start | bytes 3145736 | tf_op jit(solution)/shard_map/ppermute | solution.py:319
  660.9 44.1 %collective-permute-start.74 = (f32[128,2048]{1,0:T(8,128)}, f32[128,2048]{1,0:T(8,128)S(1)}, u32[]{:S(2)}, u32[]{:S(2)}) collective-permute-start(f32[128,2048]{1,0:T(8,128)} %fusion.84.refs_0_), channel_id=1, source_target_pairs={{0,1},{1,0},{2,3},{3,2},{4,5},{5,4},{6,7},{7,6},{8,9},{9,8},{10,11... | collective-permute-start | bytes 3145736 | tf_op jit(solution)/shard_map/ppermute | solution.py:319
  663.0 45.1 %collective-permute-start.73 = (f32[128,2048]{1,0:T(8,128)S(1)}, f32[128,2048]{1,0:T(8,128)S(1)}, u32[]{:S(2)}, u32[]{:S(2)}) collective-permute-start(f32[128,2048]{1,0:T(8,128)S(1)} %fusion.73.refs_0_), channel_id=1, source_target_pairs={{0,2},{1,3},{2,0},{3,1},{4,6},{5,7},{6,4},{7,5},{8,10},{9,11},{10,... | collective-permute-start | bytes 3145736 | tf_op jit(solution)/shard_map/ppermute | solution.py:319
  664.3 63.1 %collective-permute-start.72 = (f32[128,2048]{1,0:T(8,128)S(1)}, f32[128,2048]{1,0:T(8,128)S(1)}, u32[]{:S(2)}, u32[]{:S(2)}) collective-permute-start(f32[128,2048]{1,0:T(8,128)S(1)} %fusion.73.refs_0_), channel_id=1, source_target_pairs={{0,1},{1,0},{2,3},{3,2},{4,5},{5,4},{6,7},{7,6},{8,9},{9,8},{10,11... | collective-permute-start | bytes 3145736 | tf_op jit(solution)/shard_map/ppermute | solution.py:319
  687.2 46.3 %collective-permute-start.71 = (f32[128,1024]{1,0:T(8,128)S(1)}, f32[128,1024]{1,0:T(8,128)S(1)}, u32[]{:S(2)}, u32[]{:S(2)}) collective-permute-start(f32[128,1024]{1,0:T(8,128)S(1)} %slice.798), channel_id=1, source_target_pairs={{0,2},{1,3},{2,0},{3,1},{4,6},{5,7},{6,4},{7,5},{8,10},{9,11},{10,... | collective-permute-start | bytes 1572872 | tf_op jit(solution)/shard_map/ppermute | solution.py:319
  689.7 49.0 %collective-permute-start.70 = (f32[128,1024]{1,0:T(8,128)S(1)}, f32[128,1024]{1,0:T(8,128)S(1)}, u32[]{:S(2)}, u32[]{:S(2)}) collective-permute-start(f32[128,1024]{1,0:T(8,128)S(1)} %slice.797), channel_id=1, source_target_pairs={{0,1},{1,0},{2,3},{3,2},{4,5},{5,4},{6,7},{7,6},{8,9},{9,8},{10,11... | collective-permute-start | bytes 1572872 | tf_op jit(solution)/shard_map/ppermute | solution.py:319
  (193 other events, 3708.6 us)
Sparse Core Ops, SparseCore 0:
  481.6 131.8 reduce-scatter.4
  616.3 49.0 reduce-scatter.6
  668.3 167.4 reduce-scatter.10
  838.6 166.5 reduce-scatter.8
